TPU v7x, 512 devices: a whole 4x8x8 slice. The times are simulated.
512 devices in a mesh: node: 64 (over y, z_lo, core), local: 8 (over z_hi, x).
Axes of the slice: x: 4, y: 8, z: 8 (z_hi: 2, z_lo: 4; z = z_hi * 4 + z_lo), core: 2. Of those that a mesh axis runs over, the one named last changes fastest.
Arguments:
- hidden_acts: bfloat16 [65536, 1024], P(('node', 'local')), may hold values from -6 to 6
- out_grad: bfloat16 [65536, 4096], P(('node', 'local')), may hold values from -6 to 6
- weight: bfloat16 [32768, 4096], P('node', 'local'), may hold values from -0.1875 to 0.1875
- first_moment: bfloat16 [32768, 4096], P('node', 'local'), may hold values from -6 to 6
- second_moment: bfloat16 [32768, 4096], P('node', 'local'), may hold values from 0.5 to 8
- holder_expert: int32 [32], replicated, may hold values from 0 to 31
- new_source: int32 [32], replicated, may hold values from 0 to 31, as said below
- live_blocks: int32 [64, 8], P('node', 'local'), may hold values from 1 to 4, as said below
Outputs:
- next_weight: bfloat16 [32768, 4096], P('node', 'local')
- next_first: bfloat16 [32768, 4096], P('node', 'local')
- next_second: bfloat16 [32768, 4096], P('node', 'local')
- hidden_back: bfloat16 [65536, 1024], P(('node', 'local'))
Inputs may be any that keep to these rules, and one draw needn't show every extreme that they name: `new_source`: each entry names a copy. The live rows of a device are its first 32 * live_blocks rows.
All inputs are finite; a program needn't handle non-finite values.
Results may differ from a plain program's by a relative error of at most 0.001.
Values may be sent and summed in bfloat16 or wider, within the bound.
A program may use at most 64 MiB of HBM per device.

v0:
```python
import jax
import jax.numpy as jnp
from jax import lax
from jax.sharding import PartitionSpec as P

ROW_BLOCK = 32
beta_one = 0.9
beta_two = 0.95
learn_rate = 0.002
decay_rate = 0.1
adam_eps = 1e-08
step_count = 10.0


def swapped(block, axis, distance):
    count = lax.axis_size(axis)
    route = []
    for low in range(count):
        high = low | 1 << distance
        if high != low and high < count:
            route += [(low, high), (high, low)]
    return lax.ppermute(block, axis, route)


def shortened(array):
    return jax.tree.map(lambda a: a.astype(jnp.bfloat16) if a.dtype == jnp.float32 else a, array)


def adamw_step(gradient, weight, first, second):
    first_new = beta_one * first.astype(jnp.float32) + (1.0 - beta_one) * gradient
    second_new = beta_two * second.astype(jnp.float32) + (1.0 - beta_two) * gradient * gradient
    update = (
        first_new
        / (1.0 - beta_one**step_count)
        / (jnp.sqrt(second_new / (1.0 - beta_two**step_count)) + adam_eps)
    )
    master = weight.astype(jnp.float32)
    weight_new = master - learn_rate * (update + decay_rate * master)
    return (
        weight_new.astype(jnp.bfloat16),
        first_new.astype(jnp.bfloat16),
        second_new.astype(jnp.bfloat16),
    )


def group_total(group_blend, gradient, node_count):
    col_count = gradient.shape[1]
    stacked = gradient.reshape(node_count, -1, col_count)
    return jnp.einsum("kj,jrc->krc", group_blend, stacked, precision=lax.Precision.HIGHEST)


def shards(
    hidden_acts,
    out_grad,
    weight,
    first_moment,
    second_moment,
    holder_expert,
    new_source,
    live_blocks,
):
    tok_rows = out_grad.shape[0]
    half_rows = weight.shape[0]
    row_ids = lax.broadcasted_iota(jnp.int32, (tok_rows, 1), 0)
    live_rows = live_blocks[0, 0] * ROW_BLOCK
    masked = jnp.where(row_ids < live_rows, out_grad, jnp.zeros_like(out_grad))
    columns = lax.all_to_all(masked, "local", split_axis=1, concat_axis=0, tiled=True)
    parity = lax.axis_index("node") % 2
    partner_half = swapped(weight, "node", 0)
    full_weight = jnp.where(
        parity == 0,
        jnp.concatenate([weight, partner_half], axis=0),
        jnp.concatenate([partner_half, weight], axis=0),
    )
    row_part = columns
    grad_whole = lax.dot_general(
        lax.all_gather(hidden_acts, "local", axis=0, tiled=True),
        row_part,
        (((0,), (0,)), ((), ())),
        preferred_element_type=jnp.float32,
    )
    row_part = columns
    hidden_back = lax.psum_scatter(
        lax.dot_general(
            row_part, full_weight, (((1,), (1,)), ((), ())), preferred_element_type=jnp.float32
        ),
        "local",
        scatter_dimension=0,
        tiled=True,
    ).astype(jnp.bfloat16)
    own_part = lax.dynamic_slice_in_dim(grad_whole, parity * half_rows, half_rows, 0)
    other_part = lax.dynamic_slice_in_dim(grad_whole, (1 - parity) * half_rows, half_rows, 0)
    grad_part = own_part + swapped(other_part, "node", 0)
    node_count = lax.axis_size("node")
    node_ids = jnp.arange(node_count, dtype=jnp.int32)
    node_holder = jnp.repeat(holder_expert, 2)
    node_parity = node_ids % 2
    group_blend = (
        (node_holder[:, None] == node_holder[None, :])
        & (node_parity[:, None] == node_parity[None, :])
    ).astype(jnp.float32)
    source_node = 2 * jnp.repeat(new_source, 2) + node_parity
    pieces = lax.all_to_all(grad_part, "node", split_axis=0, concat_axis=0, tiled=True)
    col_count = pieces.shape[1]
    summed = group_total(group_blend, pieces, node_count)
    full_grad = lax.all_to_all(
        summed.reshape(-1, col_count), "node", split_axis=0, concat_axis=0, tiled=True
    )
    weight_new, first_new, second_new = adamw_step(full_grad, weight, first_moment, second_moment)
    pieces = (
        lax.all_to_all(weight_new, "node", split_axis=0, concat_axis=0, tiled=True),
        lax.all_to_all(first_new, "node", split_axis=0, concat_axis=0, tiled=True),
        lax.all_to_all(second_new, "node", split_axis=0, concat_axis=0, tiled=True),
    )
    col_count = pieces[0].shape[1]
    migrated = tuple(
        (
            jnp.take(state.reshape(node_count, -1, col_count), source_node, axis=0).reshape(
                -1, col_count
            )
            for state in pieces
        )
    )
    next_weight, next_first, next_second = jax.tree.map(
        lambda part, own: part.astype(own.dtype),
        lax.all_to_all(shortened(migrated), "node", split_axis=0, concat_axis=0, tiled=True),
        migrated,
    )
    return (next_weight, next_first, next_second, hidden_back)


def solution(mesh):
    return jax.shard_map(
        shards,
        mesh=mesh,
        in_specs=(
            P(("node", "local"), None),
            P(("node", "local"), None),
            P("node", "local"),
            P("node", "local"),
            P("node", "local"),
            P(),
            P(),
            P("node", "local"),
        ),
        out_specs=(
            P("node", "local"),
            P("node", "local"),
            P("node", "local"),
            P(("node", "local"), None),
        ),
        check_vma=False,
    )
```

profile of v0, /device:TPU:1, one launch (start us, length us, event | category | flops | bytes accessed | tf_op | source)
XLA Modules:
  0.0 386.4 jit_solution(8248881727902081018)
XLA Ops:
  8.5 1.6 copy.21
  10.2 1.1 broadcast_select_fusion
  11.2 13.3 %all-to-all-start = ((bf16[128,8,512]{0,2,1:T(8,128)(2,1)}), bf16[128,8,512]{0,2,1:T(8,128)(2,1)S(1)}, u32[]{:S(2)}, u32[]{:S(2)}) async-start(bf16[128,8,512]{0,2,1:T(8,128)(2,1)} %bitcast.2), calls=%async_computation | async-start | bytes 2097152 | tf_op jit(solution)/shard_map/all_to_all | solution.py:67
  24.5 18.6 %all-to-all-done = bf16[128,8,512]{0,2,1:T(8,128)(2,1)S(1)} async-done(((bf16[128,8,512]{0,2,1:T(8,128)(2,1)}), bf16[128,8,512]{0,2,1:T(8,128)(2,1)S(1)}, u32[]{:S(2)}, u32[]{:S(2)}) %all-to-all-start) | async-done | bytes 1048608 | tf_op jit(solution)/shard_map/all_to_all | solution.py:67
  43.7 65.6 %all-gather.2.cloned.1.call-done = bf16[1024,1024]{1,0:T(8,128)(2,1)} async-done(((bf16[128,1024]{1,0:T(8,128)(2,1)}), bf16[1024,1024]{1,0:T(8,128)(2,1)}) %all-gather.2.cloned.1.call-update) | async-done | bytes 2097168 | tf_op jit(solution)/shard_map/all_gather | solution.py:77
  109.3 2.9 fusion.28
  112.1 1.1 dynamic-slice_bitcast_fusion
  113.2 4.1 %collective-permute-start = (f32[512,512]{0,1:T(8,128)}, f32[512,512]{0,1:T(8,128)}, u32[]{:S(2)}, u32[]{:S(2)}) collective-permute-start(f32[512,512]{0,1:T(8,128)} %dynamic-slice_bitcast_fusion), channel_id=1, source_target_pairs={{0,8},{8,0},{16,24},{24,16},{32,40},{40,32},{48,56},{56,48},{64,72... | collective-permute-start | bytes 3145736 | tf_op jit(solution)/shard_map/ppermute | solution.py:22
  117.4 2.6 collective-permute-done
  120.0 2.4 bitcast_add_fusion
  122.4 2.6 copy.23
  125.0 8.1 %all-to-all-start.1 = ((f32[64,8,512]{2,1,0:T(8,128)}), f32[64,8,512]{2,1,0:T(8,128)S(1)}, u32[]{:S(2)}, u32[]{:S(2)}) async-start(f32[64,8,512]{2,1,0:T(8,128)} %bitcast.7), calls=%async_computation.1 | async-start | bytes 2097152 | tf_op jit(solution)/shard_map/all_to_all | solution.py:103
  133.1 2.4 collective-permute-start.1
  135.7 26.0 %all-to-all-done.1 = f32[64,8,512]{2,1,0:T(8,128)S(1)} async-done(((f32[64,8,512]{2,1,0:T(8,128)}), f32[64,8,512]{2,1,0:T(8,128)S(1)}, u32[]{:S(2)}, u32[]{:S(2)}) %all-to-all-start.1) | async-done | bytes 1048608 | tf_op jit(solution)/shard_map/all_to_all | solution.py:103
  161.6 1.3 fusion.11
  162.9 1.6 copy.25
  164.5 6.0 %all-to-all-start.2 = ((f32[64,8,512]{2,1,0:T(8,128)}), f32[64,8,512]{2,1,0:T(8,128)S(1)}, u32[]{:S(2)}, u32[]{:S(2)}) async-start(f32[64,8,512]{2,1,0:T(8,128)} %copy.25), calls=%async_computation.2 | async-start | bytes 2097152 | tf_op jit(solution)/shard_map/all_to_all | solution.py:106
  170.6 4.4 %fusion.4 = f32[1024,1024]{1,0:T(8,128)} fusion(bf16[1024,512]{1,0:T(8,128)(2,1)S(1)} %bitcast.44, bf16[512,512]{1,0:T(8,128)(2,1)} %collective-permute-done.1, bf16[512,512]{1,0:T(8,128)(2,1)S(1)} %copy-done.2, pred[]{:T(512)S(6)} %eq.42), kind=kOutput, calls=%fused_computation.11 | convolution fusion | flops 1078460416 | bytes 6291457 | tf_op jit(solution)/shard_map/dot_general | solution.py:84
  175.0 25.2 %all-to-all-done.2 = f32[64,8,512]{2,1,0:T(8,128)S(1)} async-done(((f32[64,8,512]{2,1,0:T(8,128)}), f32[64,8,512]{2,1,0:T(8,128)S(1)}, u32[]{:S(2)}, u32[]{:S(2)}) %all-to-all-start.2) | async-done | bytes 1048608 | tf_op jit(solution)/shard_map/all_to_all | solution.py:106
  200.2 1.8 fusion.16
  202.0 42.0 %all_to_all.91 = bf16[64,8,512]{2,1,0:T(8,128)(2,1)S(1)} all-to-all(bf16[64,8,512]{2,1,0:T(8,128)(2,1)S(1)} %get-tuple-element.7), channel_id=1, replica_groups=mesh['node'=64,'local'=8] {'node'}, dimensions={0} | all-to-all | bytes 1048576 | tf_op jit(solution)/shard_map/all_to_all | solution.py:113
  244.0 25.3 %all_to_all.92 = bf16[64,8,512]{2,1,0:T(8,128)(2,1)S(1)} all-to-all(bf16[64,8,512]{2,1,0:T(8,128)(2,1)S(1)} %get-tuple-element.8), channel_id=1, replica_groups=mesh['node'=64,'local'=8] {'node'}, dimensions={0} | all-to-all | bytes 1048576 | tf_op jit(solution)/shard_map/all_to_all | solution.py:111
  269.3 16.3 %all-to-all-start.5 = ((bf16[64,8,512]{2,1,0:T(8,128)(2,1)}), bf16[64,8,512]{2,1,0:T(8,128)(2,1)S(1)}, u32[]{:S(2)}, u32[]{:S(2)}) async-start(bf16[64,8,512]{2,1,0:T(8,128)(2,1)} %get-tuple-element.9), calls=%async_computation.5 | async-start | bytes 1048576 | tf_op jit(solution)/shard_map/all_to_all | solution.py:112
  287.1 16.3 %all-to-all-done.5 = bf16[64,8,512]{2,1,0:T(8,128)(2,1)S(1)} async-done(((bf16[64,8,512]{2,1,0:T(8,128)(2,1)}), bf16[64,8,512]{2,1,0:T(8,128)(2,1)S(1)}, u32[]{:S(2)}, u32[]{:S(2)}) %all-to-all-start.5) | async-done | bytes 524320 | tf_op jit(solution)/shard_map/all_to_all | solution.py:112
  303.9 1.0 broadcast_select_fusion.1
  304.9 23.1 %all_to_all.93 = bf16[64,8,512]{2,1,0:T(8,128)(2,1)S(1)} all-to-all(bf16[64,8,512]{2,1,0:T(8,128)(2,1)S(1)} %get-tuple-element.10), channel_id=1, replica_groups=mesh['node'=64,'local'=8] {'node'}, dimensions={0} | all-to-all | bytes 1048576 | tf_op jit(solution)/shard_map/all_to_all | solution.py:126
  328.1 25.8 %all_to_all.94 = bf16[64,8,512]{2,1,0:T(8,128)(2,1)S(1)} all-to-all(bf16[64,8,512]{2,1,0:T(8,128)(2,1)S(1)} %get-tuple-element.11), channel_id=1, replica_groups=mesh['node'=64,'local'=8] {'node'}, dimensions={0} | all-to-all | bytes 1048576 | tf_op jit(solution)/shard_map/all_to_all | solution.py:126
  353.9 5.6 %all-to-all-start.4 = ((bf16[64,8,512]{2,1,0:T(8,128)(2,1)}), bf16[64,8,512]{2,1,0:T(8,128)(2,1)S(1)}, u32[]{:S(2)}, u32[]{:S(2)}) async-start(bf16[64,8,512]{2,1,0:T(8,128)(2,1)} %get-tuple-element.12), calls=%async_computation.4 | async-start | bytes 1048576 | tf_op jit(solution)/shard_map/all_to_all | solution.py:126
  359.5 1.8 convert_element_type.28
  361.3 15.9 %all-to-all-done.4 = bf16[64,8,512]{2,1,0:T(8,128)(2,1)S(1)} async-done(((bf16[64,8,512]{2,1,0:T(8,128)(2,1)}), bf16[64,8,512]{2,1,0:T(8,128)(2,1)S(1)}, u32[]{:S(2)}, u32[]{:S(2)}) %all-to-all-start.4) | async-done | bytes 524320 | tf_op jit(solution)/shard_map/all_to_all | solution.py:126
  377.2 0.8 copy.32
  378.0 0.8 copy.33
  (30 shorter events, 4.3 us)
Async XLA Ops:
  7.2 102.1 %all-gather.2.cloned.1.call-start = ((), (), s32[]{:S(2)}) async-start(), calls=%async_computation.10 | async-start | bytes 2359296 | tf_op jit(solution)/shard_map/all_gather | solution.py:77
  11.2 31.9 %all-to-all-start = ((bf16[128,8,512]{0,2,1:T(8,128)(2,1)}), bf16[128,8,512]{0,2,1:T(8,128)(2,1)S(1)}, u32[]{:S(2)}, u32[]{:S(2)}) async-start(bf16[128,8,512]{0,2,1:T(8,128)(2,1)} %bitcast.2), calls=%async_computation | async-start | bytes 2097152 | tf_op jit(solution)/shard_map/all_to_all | solution.py:67
  113.2 6.8 %collective-permute-start = (f32[512,512]{0,1:T(8,128)}, f32[512,512]{0,1:T(8,128)}, u32[]{:S(2)}, u32[]{:S(2)}) collective-permute-start(f32[512,512]{0,1:T(8,128)} %dynamic-slice_bitcast_fusion), channel_id=1, source_target_pairs={{0,8},{8,0},{16,24},{24,16},{32,40},{40,32},{48,56},{56,48},{64,72... | collective-permute-start | bytes 3145736 | tf_op jit(solution)/shard_map/ppermute | solution.py:22
  122.4 10.7 %copy-start.2 = (bf16[512,512]{1,0:T(8,128)(2,1)S(1)}, bf16[512,512]{1,0:T(8,128)(2,1)}, u32[]{:S(2)}) copy-start(bf16[512,512]{1,0:T(8,128)(2,1)} %param.12) | copy-start | bytes 1572868
  122.4 13.1 %copy-start.3 = (s32[32]{0:T(128)S(1)}, s32[32]{0:T(128)}, u32[]{:S(2)}) copy-start(s32[32]{0:T(128)} %param.15) | copy-start | bytes 388
  125.0 36.7 %all-to-all-start.1 = ((f32[64,8,512]{2,1,0:T(8,128)}), f32[64,8,512]{2,1,0:T(8,128)S(1)}, u32[]{:S(2)}, u32[]{:S(2)}) async-start(f32[64,8,512]{2,1,0:T(8,128)} %bitcast.7), calls=%async_computation.1 | async-start | bytes 2097152 | tf_op jit(solution)/shard_map/all_to_all | solution.py:103
  133.1 37.5 %collective-permute-start.1 = (bf16[512,512]{1,0:T(8,128)(2,1)S(1)}, bf16[512,512]{1,0:T(8,128)(2,1)}, u32[]{:S(2)}, u32[]{:S(2)}) collective-permute-start(bf16[512,512]{1,0:T(8,128)(2,1)S(1)} %copy-done.2), channel_id=1, source_target_pairs={{0,8},{8,0},{16,24},{24,16},{32,40},{40,32},{48,56},{56,48},{64,72... | collective-permute-start | bytes 1572872 | tf_op jit(solution)/shard_map/ppermute | solution.py:22
  164.5 35.6 %all-to-all-start.2 = ((f32[64,8,512]{2,1,0:T(8,128)}), f32[64,8,512]{2,1,0:T(8,128)S(1)}, u32[]{:S(2)}, u32[]{:S(2)}) async-start(f32[64,8,512]{2,1,0:T(8,128)} %copy.25), calls=%async_computation.2 | async-start | bytes 2097152 | tf_op jit(solution)/shard_map/all_to_all | solution.py:106
  170.5 189.0 %reduce-scatter.2.cloned.1.call-start = ((), (), s32[]{:S(2)}) async-start(), calls=%async_computation.11 | async-start | bytes 4718592 | tf_op jit(solution)/shard_map/reduce_scatter | solution.py:83
  175.0 25.2 %copy-start = (bf16[512,512]{1,0:T(8,128)(2,1)S(1)}, bf16[512,512]{1,0:T(8,128)(2,1)}, u32[]{:S(2)}) copy-start(bf16[512,512]{1,0:T(8,128)(2,1)} %param.14) | copy-start | bytes 1572868
  175.0 25.2 %copy-start.1 = (bf16[512,512]{1,0:T(8,128)(2,1)S(1)}, bf16[512,512]{1,0:T(8,128)(2,1)}, u32[]{:S(2)}) copy-start(bf16[512,512]{1,0:T(8,128)(2,1)} %param.13) | copy-start | bytes 1572868
  202.0 83.7 %copy-start.4 = (s32[32]{0:T(128)S(1)}, s32[32]{0:T(128)}, u32[]{:S(2)}) copy-start(s32[32]{0:T(128)} %param.16) | copy-start | bytes 388
  269.3 34.0 %all-to-all-start.5 = ((bf16[64,8,512]{2,1,0:T(8,128)(2,1)}), bf16[64,8,512]{2,1,0:T(8,128)(2,1)S(1)}, u32[]{:S(2)}, u32[]{:S(2)}) async-start(bf16[64,8,512]{2,1,0:T(8,128)(2,1)} %get-tuple-element.9), calls=%async_computation.5 | async-start | bytes 1048576 | tf_op jit(solution)/shard_map/all_to_all | solution.py:112
  353.9 23.3 %all-to-all-start.4 = ((bf16[64,8,512]{2,1,0:T(8,128)(2,1)}), bf16[64,8,512]{2,1,0:T(8,128)(2,1)S(1)}, u32[]{:S(2)}, u32[]{:S(2)}) async-start(bf16[64,8,512]{2,1,0:T(8,128)(2,1)} %get-tuple-element.12), calls=%async_computation.4 | async-start | bytes 1048576 | tf_op jit(solution)/shard_map/all_to_all | solution.py:126
Sparse Core Ops, SparseCore 0:
  11.2 98.0 all-gather.1
  176.1 160.2 reduce-scatter.1
where the time goes:
time: 387 us; the launch traced here: 386 us
  waiting for transfers between devices  171 us (44%)
  blocking collectives  116 us (30%)
  starting transfers between devices  55.8 us (14%)
  between operations  14.9 us (4%)
  local copies, waits for them, and re-layouts  12 us (3%)
  matrix products  8.58 us (2%)
  other arithmetic  8.06 us (2%)
    all_gather x1, waiting for transfers between devices, shards(): lax.all_gather(hidden_acts, 'local', axis=0, tiled=True)  65.6 us
    all_to_all x2, blocking collectives, shards(): lax.all_to_all(shortened(migrated), 'node', split_axis=0, concat_axis=0,...  49 us
    all_to_all x1, blocking collectives, shards(): lax.all_to_all(second_new, 'node', split_axis=0, concat_axis=0, tiled=True)  42 us
    all_to_all x1, waiting for transfers between devices, shards(): lax.all_to_all(grad_part, 'node', split_axis=0, concat_axis=0, tiled=True)  26 us
    all_to_all x1, blocking collectives, shards(): lax.all_to_all(weight_new, 'node', split_axis=0, concat_axis=0, tiled=True)  25.3 us
    all_to_all x1, waiting for transfers between devices, shards(): lax.all_to_all(summed.reshape(-1, col_count), 'node', split_axis=0, conca...  25.2 us
    all_to_all x1, waiting for transfers between devices, shards(): lax.all_to_all(masked, 'local', split_axis=1, concat_axis=0, tiled=True)  18.6 us
    all_to_all x1, starting transfers between devices, shards(): lax.all_to_all(first_new, 'node', split_axis=0, concat_axis=0, tiled=True)  16.3 us
  transfers between devices with their start and end apart: 9, of which 7 were waited for; matrix products, arithmetic and copies ran while one was open for 4% of the time, Pallas kernels for 0%

commit v1 on v0

--- a/solution.py
+++ b/solution.py
@@ -74,7 +74,9 @@
     )
     row_part = columns
     grad_whole = lax.dot_general(
-        lax.all_gather(hidden_acts, "local", axis=0, tiled=True),
+        jnp.concatenate(
+            lax.all_to_all(jnp.stack([hidden_acts] * lax.axis_size("local")), "local", 0, 0), axis=0
+        ),
         row_part,
         (((0,), (0,)), ((), ())),
         preferred_element_type=jnp.float32,

time: 387 us -> 388 us (level)
  the two profiles are of different devices: /device:TPU:1 before, /device:TPU:5 now
where the time goes in v1:
time: 388 us; the launch traced here: 387 us
  blocking collectives  160 us (41%)
  waiting for transfers between devices  105 us (27%)
  starting transfers between devices  79.6 us (21%)
  between operations  14.9 us (4%)
  local copies, waits for them, and re-layouts  11.7 us (3%)
  other arithmetic  8.46 us (2%)
  matrix products  7.32 us (2%)
    all_to_all x2, blocking collectives, shards(): lax.all_to_all(shortened(migrated), 'node', split_axis=0, concat_axis=0,...  55 us
    all_to_all x1, blocking collectives, shards(): lax.all_to_all(weight_new, 'node', split_axis=0, concat_axis=0, tiled=True)  40.8 us
    all_to_all x1, starting transfers between devices, shards(): lax.all_to_all(grad_part, 'node', split_axis=0, concat_axis=0, tiled=True)  38.4 us
    all_to_all x1, blocking collectives, shards(): lax.all_to_all(second_new, 'node', split_axis=0, concat_axis=0, tiled=True)  35.3 us
    all_to_all x1, blocking collectives, shards(): lax.all_to_all(masked, 'local', split_axis=1, concat_axis=0, tiled=True)  29.1 us
    all_to_all x1, waiting for transfers between devices, shards(): lax.all_to_all(grad_part, 'node', split_axis=0, concat_axis=0, tiled=True)  26 us
    all_to_all x1, waiting for transfers between devices, shards(): lax.all_to_all(summed.reshape(-1, col_count), 'node', split_axis=0, conca...  23.6 us
    all_to_all x1, waiting for transfers between devices, shards(): lax.all_to_all(jnp.stack([hidden_acts] * lax.axis_size('local')), 'local'...  20.1 us
  transfers between devices with their start and end apart: 8, of which 6 were waited for; matrix products, arithmetic and copies ran while one was open for 4% of the time, Pallas kernels for 0%

profile of v1, /device:TPU:5, one launch (start us, length us, event | category | flops | bytes accessed | tf_op | source)
XLA Modules:
  0.0 387.0 jit_solution(4430717616407658378)
XLA Ops:
  7.8 1.4 broadcast_select_fusion
  9.9 29.1 %all_to_all.96 = bf16[128,8,512]{0,2,1:T(8,128)(2,1)S(1)} all-to-all(bf16[128,8,512]{0,2,1:T(8,128)(2,1)S(1)} %bitcast.47), channel_id=1, replica_groups=mesh['node'=64,'local'=8] {'local'}, dimensions={1} | all-to-all | bytes 2097152 | tf_op jit(solution)/shard_map/all_to_all | solution.py:67
  39.0 1.6 stack.2
  40.6 5.1 %all-to-all-start.1 = ((bf16[8,128,1024]{2,1,0:T(8,128)(2,1)}), bf16[8,128,1024]{2,1,0:T(8,128)(2,1)S(1)}, u32[]{:S(2)}, u32[]{:S(2)}) async-start(bf16[8,128,1024]{2,1,0:T(8,128)(2,1)} %stack.2), calls=%async_computation.1 | async-start | bytes 4194304 | tf_op jit(solution)/shard_map/all_to_all | solution.py:78
  45.7 20.1 %all-to-all-done.1 = bf16[8,128,1024]{2,1,0:T(8,128)(2,1)S(1)} async-done(((bf16[8,128,1024]{2,1,0:T(8,128)(2,1)}), bf16[8,128,1024]{2,1,0:T(8,128)(2,1)S(1)}, u32[]{:S(2)}, u32[]{:S(2)}) %all-to-all-start.1) | async-done | bytes 2097184 | tf_op jit(solution)/shard_map/all_to_all | solution.py:78
  65.7 1.2 convolution_bitcast_fusion
  67.0 1.3 copy-done
  68.4 12.6 %collective-permute-start = (f32[512,512]{0,1:T(8,128)S(1)}, f32[512,512]{0,1:T(8,128)S(1)}, u32[]{:S(2)}, u32[]{:S(2)}) collective-permute-start(f32[512,512]{0,1:T(8,128)S(1)} %dynamic-slice_bitcast_fusion), channel_id=1, source_target_pairs={{0,8},{8,0},{16,24},{24,16},{32,40},{40,32},{48,56},{56,48},{64,72... | collective-permute-start | bytes 3145736 | tf_op jit(solution)/shard_map/ppermute | solution.py:22
  81.1 2.3 collective-permute-done
  83.3 1.4 bitcast_add_fusion
  84.8 1.3 copy.20
  86.1 38.4 %all-to-all-start.2 = ((f32[64,8,512]{2,1,0:T(8,128)}), f32[64,8,512]{2,1,0:T(8,128)S(1)}, u32[]{:S(2)}, u32[]{:S(2)}) async-start(f32[64,8,512]{2,1,0:T(8,128)} %bitcast.7), calls=%async_computation.2 | async-start | bytes 2097152 | tf_op jit(solution)/shard_map/all_to_all | solution.py:105
  124.5 2.4 collective-permute-start.1
  127.0 26.0 %all-to-all-done.2 = f32[64,8,512]{2,1,0:T(8,128)S(1)} async-done(((f32[64,8,512]{2,1,0:T(8,128)}), f32[64,8,512]{2,1,0:T(8,128)S(1)}, u32[]{:S(2)}, u32[]{:S(2)}) %all-to-all-start.2) | async-done | bytes 1048608 | tf_op jit(solution)/shard_map/all_to_all | solution.py:105
  153.0 1.3 fusion.11
  154.3 1.6 copy.22
  155.9 6.0 %all-to-all-start.3 = ((f32[64,8,512]{2,1,0:T(8,128)}), f32[64,8,512]{2,1,0:T(8,128)S(1)}, u32[]{:S(2)}, u32[]{:S(2)}) async-start(f32[64,8,512]{2,1,0:T(8,128)} %copy.22), calls=%async_computation.3 | async-start | bytes 2097152 | tf_op jit(solution)/shard_map/all_to_all | solution.py:108
  162.5 4.8 %fusion.4 = f32[1024,1024]{1,0:T(8,128)} fusion(bf16[1024,512]{1,0:T(8,128)(2,1)S(1)} %bitcast.51, bf16[512,512]{1,0:T(8,128)(2,1)} %collective-permute-done.1, bf16[512,512]{1,0:T(8,128)(2,1)} %param.12, pred[]{:T(512)S(6)} %eq.42), kind=kOutput, calls=%fused_computation.12 | convolution fusion | flops 1078460416 | bytes 6291457 | tf_op jit(solution)/shard_map/dot_general | solution.py:86
  167.3 23.6 %all-to-all-done.3 = f32[64,8,512]{2,1,0:T(8,128)S(1)} async-done(((f32[64,8,512]{2,1,0:T(8,128)}), f32[64,8,512]{2,1,0:T(8,128)S(1)}, u32[]{:S(2)}, u32[]{:S(2)}) %all-to-all-start.3) | async-done | bytes 1048608 | tf_op jit(solution)/shard_map/all_to_all | solution.py:108
  190.9 2.8 fusion.16
  193.8 35.3 %all_to_all.97 = bf16[64,8,512]{2,1,0:T(8,128)(2,1)S(1)} all-to-all(bf16[64,8,512]{2,1,0:T(8,128)(2,1)S(1)} %get-tuple-element.7), channel_id=1, replica_groups=mesh['node'=64,'local'=8] {'node'}, dimensions={0} | all-to-all | bytes 1048576 | tf_op jit(solution)/shard_map/all_to_all | solution.py:115
  229.0 40.8 %all_to_all.98 = bf16[64,8,512]{2,1,0:T(8,128)(2,1)S(1)} all-to-all(bf16[64,8,512]{2,1,0:T(8,128)(2,1)S(1)} %get-tuple-element.8), channel_id=1, replica_groups=mesh['node'=64,'local'=8] {'node'}, dimensions={0} | all-to-all | bytes 1048576 | tf_op jit(solution)/shard_map/all_to_all | solution.py:113
  269.8 9.6 %all-to-all-start.6 = ((bf16[64,8,512]{2,1,0:T(8,128)(2,1)}), bf16[64,8,512]{2,1,0:T(8,128)(2,1)S(1)}, u32[]{:S(2)}, u32[]{:S(2)}) async-start(bf16[64,8,512]{2,1,0:T(8,128)(2,1)} %get-tuple-element.9), calls=%async_computation.6 | async-start | bytes 1048576 | tf_op jit(solution)/shard_map/all_to_all | solution.py:114
  280.9 17.0 %all-to-all-done.6 = bf16[64,8,512]{2,1,0:T(8,128)(2,1)S(1)} async-done(((bf16[64,8,512]{2,1,0:T(8,128)(2,1)}), bf16[64,8,512]{2,1,0:T(8,128)(2,1)S(1)}, u32[]{:S(2)}, u32[]{:S(2)}) %all-to-all-start.6) | async-done | bytes 524320 | tf_op jit(solution)/shard_map/all_to_all | solution.py:114
  298.5 1.0 broadcast_select_fusion.1
  299.5 32.0 %all_to_all.99 = bf16[64,8,512]{2,1,0:T(8,128)(2,1)S(1)} all-to-all(bf16[64,8,512]{2,1,0:T(8,128)(2,1)S(1)} %get-tuple-element.10), channel_id=1, replica_groups=mesh['node'=64,'local'=8] {'node'}, dimensions={0} | all-to-all | bytes 1048576 | tf_op jit(solution)/shard_map/all_to_all | solution.py:128
  331.4 23.1 %all_to_all.100 = bf16[64,8,512]{2,1,0:T(8,128)(2,1)S(1)} all-to-all(bf16[64,8,512]{2,1,0:T(8,128)(2,1)S(1)} %get-tuple-element.11), channel_id=1, replica_groups=mesh['node'=64,'local'=8] {'node'}, dimensions={0} | all-to-all | bytes 1048576 | tf_op jit(solution)/shard_map/all_to_all | solution.py:128
  354.5 5.6 %all-to-all-start.5 = ((bf16[64,8,512]{2,1,0:T(8,128)(2,1)}), bf16[64,8,512]{2,1,0:T(8,128)(2,1)S(1)}, u32[]{:S(2)}, u32[]{:S(2)}) async-start(bf16[64,8,512]{2,1,0:T(8,128)(2,1)} %get-tuple-element.12), calls=%async_computation.5 | async-start | bytes 1048576 | tf_op jit(solution)/shard_map/all_to_all | solution.py:128
  360.1 1.8 convert_element_type.28
  361.9 15.9 %all-to-all-done.5 = bf16[64,8,512]{2,1,0:T(8,128)(2,1)S(1)} async-done(((bf16[64,8,512]{2,1,0:T(8,128)(2,1)}), bf16[64,8,512]{2,1,0:T(8,128)(2,1)S(1)}, u32[]{:S(2)}, u32[]{:S(2)}) %all-to-all-start.5) | async-done | bytes 524320 | tf_op jit(solution)/shard_map/all_to_all | solution.py:128
  377.8 0.8 copy.30
  379.4 0.8 copy.32
  (31 shorter events, 4.3 us)
Async XLA Ops:
  9.2 29.8 %copy-start.3 = (bf16[128,1024]{1,0:T(8,128)(2,1)S(1)}, bf16[128,1024]{1,0:T(8,128)(2,1)}, u32[]{:S(2)}) copy-start(bf16[128,1024]{1,0:T(8,128)(2,1)} %param.10) | copy-start | bytes 786436
  40.6 25.2 %all-to-all-start.1 = ((bf16[8,128,1024]{2,1,0:T(8,128)(2,1)}), bf16[8,128,1024]{2,1,0:T(8,128)(2,1)S(1)}, u32[]{:S(2)}, u32[]{:S(2)}) async-start(bf16[8,128,1024]{2,1,0:T(8,128)(2,1)} %stack.2), calls=%async_computation.1 | async-start | bytes 4194304 | tf_op jit(solution)/shard_map/all_to_all | solution.py:78
  67.0 1.3 copy-start
  68.4 14.9 %collective-permute-start = (f32[512,512]{0,1:T(8,128)S(1)}, f32[512,512]{0,1:T(8,128)S(1)}, u32[]{:S(2)}, u32[]{:S(2)}) collective-permute-start(f32[512,512]{0,1:T(8,128)S(1)} %dynamic-slice_bitcast_fusion), channel_id=1, source_target_pairs={{0,8},{8,0},{16,24},{24,16},{32,40},{40,32},{48,56},{56,48},{64,72... | collective-permute-start | bytes 3145736 | tf_op jit(solution)/shard_map/ppermute | solution.py:22
  84.7 42.1 %copy-start.4 = (s32[32]{0:T(128)S(1)}, s32[32]{0:T(128)}, u32[]{:S(2)}) copy-start(s32[32]{0:T(128)} %param.15) | copy-start | bytes 388
  86.1 66.9 %all-to-all-start.2 = ((f32[64,8,512]{2,1,0:T(8,128)}), f32[64,8,512]{2,1,0:T(8,128)S(1)}, u32[]{:S(2)}, u32[]{:S(2)}) async-start(f32[64,8,512]{2,1,0:T(8,128)} %bitcast.7), calls=%async_computation.2 | async-start | bytes 2097152 | tf_op jit(solution)/shard_map/all_to_all | solution.py:105
  124.5 38.0 %collective-permute-start.1 = (bf16[512,512]{1,0:T(8,128)(2,1)}, bf16[512,512]{1,0:T(8,128)(2,1)}, u32[]{:S(2)}, u32[]{:S(2)}) collective-permute-start(bf16[512,512]{1,0:T(8,128)(2,1)} %param.12), channel_id=1, source_target_pairs={{0,8},{8,0},{16,24},{24,16},{32,40},{40,32},{48,56},{56,48},{64,72... | collective-permute-start | bytes 1572872 | tf_op jit(solution)/shard_map/ppermute | solution.py:22
  155.9 35.0 %all-to-all-start.3 = ((f32[64,8,512]{2,1,0:T(8,128)}), f32[64,8,512]{2,1,0:T(8,128)S(1)}, u32[]{:S(2)}, u32[]{:S(2)}) async-start(f32[64,8,512]{2,1,0:T(8,128)} %copy.22), calls=%async_computation.3 | async-start | bytes 2097152 | tf_op jit(solution)/shard_map/all_to_all | solution.py:108
  161.9 198.2 %reduce-scatter.2.cloned.1.call-start = ((), (), s32[]{:S(2)}) async-start(), calls=%async_computation.11 | async-start | bytes 4718592 | tf_op jit(solution)/shard_map/reduce_scatter | solution.py:85
  167.2 23.7 %copy-start.1 = (bf16[512,512]{1,0:T(8,128)(2,1)S(1)}, bf16[512,512]{1,0:T(8,128)(2,1)}, u32[]{:S(2)}) copy-start(bf16[512,512]{1,0:T(8,128)(2,1)} %param.14) | copy-start | bytes 1572868
  167.3 23.7 %copy-start.2 = (bf16[512,512]{1,0:T(8,128)(2,1)S(1)}, bf16[512,512]{1,0:T(8,128)(2,1)}, u32[]{:S(2)}) copy-start(bf16[512,512]{1,0:T(8,128)(2,1)} %param.13) | copy-start | bytes 1572868
  193.8 85.7 %copy-start.5 = (s32[32]{0:T(128)S(1)}, s32[32]{0:T(128)}, u32[]{:S(2)}) copy-start(s32[32]{0:T(128)} %param.16) | copy-start | bytes 388
  269.8 28.0 %all-to-all-start.6 = ((bf16[64,8,512]{2,1,0:T(8,128)(2,1)}), bf16[64,8,512]{2,1,0:T(8,128)(2,1)S(1)}, u32[]{:S(2)}, u32[]{:S(2)}) async-start(bf16[64,8,512]{2,1,0:T(8,128)(2,1)} %get-tuple-element.9), calls=%async_computation.6 | async-start | bytes 1048576 | tf_op jit(solution)/shard_map/all_to_all | solution.py:114
  354.5 23.3 %all-to-all-start.5 = ((bf16[64,8,512]{2,1,0:T(8,128)(2,1)}), bf16[64,8,512]{2,1,0:T(8,128)(2,1)S(1)}, u32[]{:S(2)}, u32[]{:S(2)}) async-start(bf16[64,8,512]{2,1,0:T(8,128)(2,1)} %get-tuple-element.12), calls=%async_computation.5 | async-start | bytes 1048576 | tf_op jit(solution)/shard_map/all_to_all | solution.py:128
Sparse Core Ops, SparseCore 0:
  167.4 155.1 reduce-scatter.1
